TPU v7x, 128 devices: a whole 4x4x4 slice. The times are simulated.
128 devices in a mesh: zone: 32 (over y, x, core), sub: 4 (over z).
Axes of the slice: x: 4, y: 4, z: 4, core: 2. Of those that a mesh axis runs over, the one named last changes fastest.
Arguments:
- order_features: bfloat16 [262144, 128], P('zone'), may hold values from -6 to 6
- w_in: bfloat16 [128, 512], replicated, may hold values from -0.5 to 0.5
- bias_in: float32 [512], replicated, may hold values from -3 to 3
- w_out: bfloat16 [512, 128], replicated, may hold values from -0.25 to 0.25
- bias_out: float32 [128], replicated, may hold values from -3 to 3
- courier_embed: bfloat16 [65536, 128], P(('zone', 'sub')), may hold values from -28 to 28
- courier_cap: bfloat16 [65536], P(('zone', 'sub')), may hold values from 0.5 to 4
- adjacency: int32 [512, 8], P('zone'), may hold values from 0 to 127, all different within a row; in each aligned block of 16 rows (0 to 15, 16 to 31, ...) at most 2 rows name the same one
- order_count: int32 [512], P('zone'), may hold values from 64 to 512
- courier_count: int32 [128], P(('zone', 'sub')), may hold values from 64 to 512
Outputs:
- order_potentials: float32 [262144], P('zone')
- courier_potentials: float32 [65536], P(('zone', 'sub'))
Inputs may be any that keep to these rules, and one draw needn't show every extreme that they name: `adjacency`: each row names 8 different courier blocks and every courier block is named by some row. Among the 16 rows of one index of zone (aligned blocks of rows), no courier block is named by more than 2 rows, and in some of them one is named by exactly 2.
All inputs are finite; a program needn't handle non-finite values.
Results may differ from a plain program's by a relative error of at most 0.0017.
Values may be sent and summed in bfloat16 or wider, within the bound.
No kernel may reach another device: no remote copies, remote signals or barrier semaphores. Data moves between devices by JAX's collectives and lax.ppermute only.
A program may use at most 128 MiB of HBM per device.

v0:
```python
import math

import jax
import jax.numpy as jnp
from jax import lax
from jax.sharding import PartitionSpec as P

BLOCK = 512
EMB = 128
ADJ = 8
SWEEPS = 2
OB_DEV = 16
CB_DEV = 1


SOFTMAX_TEMPER = 0.2
LOWEST = -1e30


def combined_all(value, axis, join):
    pieces = jax.tree.map(lambda part: lax.all_gather(part, axis), value)
    head = jax.tree.map(lambda part: part[0], pieces)
    tail = jax.tree.map(lambda part: part[1:], pieces)
    running, _ = lax.scan(lambda running, piece: (join(running, piece), None), head, tail)
    return running


def embed_orders(features, w_in, bias_in, w_out, bias_out):
    hidden = jnp.dot(features, w_in, preferred_element_type=jnp.float32) + bias_in
    hidden = jax.nn.silu(hidden).astype(jnp.bfloat16)
    result = jnp.dot(hidden, w_out, preferred_element_type=jnp.float32) + bias_out
    return result.astype(jnp.bfloat16)


def join_parts(former, latter):
    peak_score_value = jnp.maximum(former[0], latter[0])
    total_weight_mass = former[1] * jnp.exp(former[0] - peak_score_value) + latter[1] * jnp.exp(
        latter[0] - peak_score_value
    )
    return (peak_score_value, total_weight_mass)


def fold_slots(running_highest, summed_terms, axes):
    peak_score_value = jnp.max(running_highest, axis=axes, keepdims=True)
    total_weight_mass = jnp.sum(
        summed_terms * jnp.exp(running_highest - peak_score_value), axis=axes
    )
    return (jnp.squeeze(peak_score_value, axis=axes), total_weight_mass)


def slot_table(adjacency, zone_count, sub_count, sub_index, per_source):
    flat_ids = adjacency.reshape(-1)
    pair_count = flat_ids.shape[0]
    pair_order = jnp.arange(pair_count, dtype=jnp.int32)
    order_of_pair = pair_order // ADJ
    same_id = flat_ids[:, None] == flat_ids[None, :]
    earlier = pair_order[None, :] < pair_order[:, None]
    rank_of = jnp.sum(same_id & earlier, axis=1)
    slot_ids = jnp.arange(zone_count * CB_DEV * per_source, dtype=jnp.int32)
    zone_of = slot_ids // (CB_DEV * per_source)
    local_of = slot_ids // per_source % CB_DEV
    place_of = slot_ids % per_source
    wanted = (zone_of * sub_count + sub_index) * CB_DEV + local_of
    matched = (wanted[:, None] == flat_ids[None, :]) & (place_of[:, None] == rank_of[None, :])
    filled = jnp.any(matched, axis=1)
    source = jnp.sum(jnp.where(matched, order_of_pair[None, :], 0), axis=1)
    return (source, filled)


def tile_pass(order_tiles, order_mask, courier_tiles, courier_mask, duals, by_rows):
    slot_count = order_tiles.shape[0]
    group_width = 8
    groups = slot_count // group_width
    inputs = (
        order_tiles.reshape(groups, group_width, BLOCK, EMB),
        order_mask.reshape(groups, group_width, BLOCK),
        courier_tiles.reshape(groups, group_width, BLOCK, EMB),
        courier_mask.reshape(groups, group_width, BLOCK),
        duals.reshape(groups, group_width, BLOCK),
    )
    affinity_scale = 1.0 / math.sqrt(EMB)

    def one_group(packed):
        order_part, order_keep, courier_part, courier_keep, partial_potential = packed
        match_affinity = (
            jnp.einsum("tie,tje->tij", order_part, courier_part, preferred_element_type=jnp.float32)
            * affinity_scale
        )
        if by_rows:
            pair_scores = (partial_potential[:, None, :] + match_affinity) / SOFTMAX_TEMPER
            usable = jnp.broadcast_to(courier_keep[:, None, :], pair_scores.shape)
            axis_used = 2
        else:
            pair_scores = (partial_potential[:, :, None] + match_affinity) / SOFTMAX_TEMPER
            usable = jnp.broadcast_to(order_keep[:, :, None], pair_scores.shape)
            axis_used = 1
        running_highest = jnp.max(
            jnp.where(usable, pair_scores, LOWEST), axis=axis_used, keepdims=True
        )
        summed_terms = jnp.sum(
            jnp.where(usable, jnp.exp(pair_scores - running_highest), 0.0), axis=axis_used
        )
        return (jnp.squeeze(running_highest, axis=axis_used), summed_terms)

    running_highest, summed_terms = lax.map(one_group, inputs)
    return (running_highest.reshape(slot_count, BLOCK), summed_terms.reshape(slot_count, BLOCK))


def settle_orders(running_highest, summed_terms, source, filled, order_active):
    chosen = (source[None, :] == jnp.arange(OB_DEV, dtype=jnp.int32)[:, None]) & filled[None, :]
    peak_score_value = jnp.max(jnp.where(chosen[:, :, None], running_highest[None], LOWEST), axis=1)
    total_weight_mass = jnp.sum(
        jnp.where(
            chosen[:, :, None],
            summed_terms[None] * jnp.exp(running_highest[None] - peak_score_value[:, None, :]),
            0.0,
        ),
        axis=1,
    )
    peak_score_value, total_weight_mass = combined_all(
        (peak_score_value, total_weight_mass), "sub", join_parts
    )
    return jnp.where(
        order_active, -SOFTMAX_TEMPER * (peak_score_value + jnp.log(total_weight_mass)), 0.0
    )


def shards(
    order_features,
    w_in,
    bias_in,
    w_out,
    bias_out,
    courier_embed,
    courier_cap,
    adjacency,
    order_count,
    courier_count,
):
    zone_count = lax.axis_size("zone")
    sub_count = lax.axis_size("sub")
    sub_index = lax.axis_index("sub")
    per_source = 2 * ADJ * OB_DEV // (sub_count * CB_DEV * zone_count)
    slot_count = zone_count * CB_DEV * per_source
    order_embed = embed_orders(order_features, w_in, bias_in, w_out, bias_out)
    order_blocks = order_embed.reshape(OB_DEV, BLOCK, EMB)
    positions = jnp.arange(BLOCK, dtype=jnp.int32)
    order_active = positions[None, :] < order_count[:, None]
    courier_active = positions[None, :] < courier_count[:, None]
    source, filled = slot_table(adjacency, zone_count, sub_count, sub_index, per_source)
    slot_order_mask = order_active[source] & filled[:, None]
    slot_range = jnp.arange(slot_count, dtype=jnp.int32)
    sent = (
        order_blocks[source].reshape(zone_count, CB_DEV * per_source, BLOCK, EMB),
        slot_order_mask.astype(jnp.bfloat16).reshape(zone_count, CB_DEV * per_source, BLOCK),
    )
    got_embed, got_mask = (
        lax.all_to_all(sent[0], "zone", split_axis=0, concat_axis=0, tiled=True),
        lax.all_to_all(sent[1], "zone", split_axis=0, concat_axis=0, tiled=True),
    )
    got_embed = got_embed.reshape(slot_count, BLOCK, EMB)
    got_mask = got_mask.reshape(slot_count, BLOCK) > 0.5
    courier_blocks = courier_embed.reshape(CB_DEV, BLOCK, EMB)
    local_block = slot_range // per_source % CB_DEV
    slot_couriers = courier_blocks[local_block]
    tile_courier_mask = courier_active[local_block]
    log_capacity = jnp.log(courier_cap.astype(jnp.float32)).reshape(CB_DEV, BLOCK)
    courier_potentials = jnp.zeros((CB_DEV, BLOCK), jnp.float32)
    order_potentials = jnp.zeros((OB_DEV, BLOCK), jnp.float32)
    for sweep_step in range(SWEEPS):
        running_highest, summed_terms = tile_pass(
            got_embed,
            got_mask,
            slot_couriers,
            tile_courier_mask,
            courier_potentials[local_block],
            True,
        )
        back_high, back_sum = (
            lax.all_to_all(
                running_highest.reshape(zone_count, CB_DEV * per_source, BLOCK),
                "zone",
                split_axis=0,
                concat_axis=0,
                tiled=True,
            ),
            lax.all_to_all(
                summed_terms.reshape(zone_count, CB_DEV * per_source, BLOCK),
                "zone",
                split_axis=0,
                concat_axis=0,
                tiled=True,
            ),
        )
        order_potentials = settle_orders(
            back_high.reshape(slot_count, BLOCK),
            back_sum.reshape(slot_count, BLOCK),
            source,
            filled,
            order_active,
        )
        got_dual = lax.all_to_all(
            order_potentials[source].reshape(zone_count, CB_DEV * per_source, BLOCK),
            "zone",
            split_axis=0,
            concat_axis=0,
            tiled=True,
        ).reshape(slot_count, BLOCK)
        running_highest, summed_terms = tile_pass(
            got_embed, got_mask, slot_couriers, tile_courier_mask, got_dual, False
        )
        peak_score_value, total_weight_mass = fold_slots(
            running_highest.reshape(zone_count, CB_DEV, per_source, BLOCK),
            summed_terms.reshape(zone_count, CB_DEV, per_source, BLOCK),
            (0, 2),
        )
        courier_potentials = jnp.where(
            courier_active,
            SOFTMAX_TEMPER * log_capacity
            - SOFTMAX_TEMPER * (peak_score_value + jnp.log(total_weight_mass)),
            0.0,
        )
    courier_out = courier_potentials.reshape(-1)
    return (order_potentials.reshape(-1), courier_out)


def solution(mesh):
    return jax.shard_map(
        shards,
        mesh=mesh,
        in_specs=(
            P("zone", None),
            P(),
            P(),
            P(),
            P(),
            P(("zone", "sub"), None),
            P(("zone", "sub")),
            P("zone", None),
            P("zone"),
            P(("zone", "sub")),
        ),
        out_specs=(P("zone"), P(("zone", "sub"))),
        check_vma=False,
    )
```

profile of v0, /device:TPU:1, one launch (start us, length us, event | category | flops | bytes accessed | tf_op | source)
XLA Modules:
  0.0 454.8 jit_solution(12190123670103468993)
XLA Ops:
  2.2 8.9 %fusion.28 = bf16[8192,128]{1,0:T(8,128)(2,1)} fusion(bf16[512,128]{1,0:T(8,128)(2,1)} %param.25, bf16[8192,128]{1,0:T(8,128)(2,1)S(1)} %copy-done, bf16[128,512]{1,0:T(8,128)(2,1)} %param.23, f32[512]{0:T(512)} %param.24, f32[128]{0:T(128)} %param.26), kind=kOutput, calls=%fused_computation.66 | convolution fusion | flops 2174746624 | bytes 4459008 | tf_op jit(solution)/shard_map/dot_general | solution.py:31
  11.2 7.0 %gather_fusion.1 = bf16[64,512,128]{2,1,0:T(8,128)(2,1)} fusion(bf16[16,512,128]{2,1,0:T(8,128)(2,1)} %bitcast.157, s32[1024]{0:T(1024)S(1)} %pad_clamp_fusion), kind=kCustom, calls=%fused_computation.1 | custom fusion | bytes 16777472 | tf_op jit(solution)/shard_map/gather | solution.py:154
  18.2 8.8 %all-to-all-start.1 = ((bf16[32,2,512,128]{3,2,1,0:T(8,128)(2,1)}), bf16[32,2,512,128]{3,2,1,0:T(8,128)(2,1)}, u32[]{:S(2)}, u32[]{:S(2)}) async-start(bf16[32,2,512,128]{3,2,1,0:T(8,128)(2,1)} %bitcast.158), calls=%async_computation.1 | async-start | bytes 16777216 | tf_op jit(solution)/shard_map/all_to_all | solution.py:158
  29.5 97.2 %all-to-all-done.1 = bf16[32,2,512,128]{3,2,1,0:T(8,128)(2,1)} async-done(((bf16[32,2,512,128]{3,2,1,0:T(8,128)(2,1)}), bf16[32,2,512,128]{3,2,1,0:T(8,128)(2,1)}, u32[]{:S(2)}, u32[]{:S(2)}) %all-to-all-start.1) | async-done | bytes 8388640 | tf_op jit(solution)/shard_map/all_to_all | solution.py:158
  126.7 5.2 %broadcast.256 = bf16[8,8,512,128]{3,2,1,0:T(8,128)(2,1)} broadcast(bf16[512,128]{1,0:T(8,128)(2,1)S(1)} %copy-done.2), dimensions={2,3} | broadcast | bytes 8519680 | tf_op jit(solution)/shard_map/reshape | solution.py:77
  132.0 39.8 %while.78 = (s32[]{:T(128)}, f32[8,8,512]{2,1,0:T(8,128)S(1)}, f32[8,8,512]{2,1,0:T(8,128)S(1)}, pred[8,8,512]{2,1,0:T(8,128)(4,1)S(1)}, bf16[8,8,512,128]{3,2,1...) while((s32[]{:T(128)}, f32[8,8,512]{2,1,0:T(8,128)S(1)}, ...), condition=%wide.region_6.7_spmd.clone, body=%wide.region_3.6_spmd.sunk.clone.sunk | while | flops 551542784 | bytes 19006548 | solution.py:105
  172.4 9.9 %all-to-all-start.2 = ((f32[32,2,512]{2,1,0:T(2,128)}), f32[32,2,512]{2,1,0:T(2,128)S(1)}, u32[]{:S(2)}, u32[]{:S(2)}) async-start(f32[32,2,512]{2,1,0:T(2,128)} %reshape_reshape.29), calls=%async_computation.2 | async-start | bytes 262144 | tf_op jit(solution)/shard_map/all_to_all | solution.py:180
  183.1 7.0 %all-to-all-done.2 = f32[32,2,512]{2,1,0:T(2,128)S(1)} async-done(((f32[32,2,512]{2,1,0:T(2,128)}), f32[32,2,512]{2,1,0:T(2,128)S(1)}, u32[]{:S(2)}, u32[]{:S(2)}) %all-to-all-start.2) | async-done | bytes 131104 | tf_op jit(solution)/shard_map/all_to_all | solution.py:180
  190.1 3.9 all-to-all-start.3
  194.5 7.2 %all-to-all-done.3 = f32[32,2,512]{2,1,0:T(2,128)S(1)} async-done(((f32[32,2,512]{2,1,0:T(2,128)}), f32[32,2,512]{2,1,0:T(2,128)S(1)}, u32[]{:S(2)}, u32[]{:S(2)}) %all-to-all-start.3) | async-done | bytes 131104 | tf_op jit(solution)/shard_map/all_to_all | solution.py:187
  206.4 11.3 %all-gather.1 = f32[64,512]{1,0:T(8,128)S(1)} all-gather(f32[16,512]{1,0:T(8,128)S(1)} %select_reduce_fusion.10), channel_id=3, replica_groups=mesh['zone'=32,'sub'=4] {'sub'}, dimensions={0}, use_global_device_ids=true | all-gather | bytes 163840 | tf_op jit(solution)/shard_map/all_gather | solution.py:21
  217.7 9.1 %all-gather = f32[64,512]{1,0:T(8,128)S(1)} all-gather(f32[16,512]{1,0:T(8,128)S(1)} %select_reduce_fusion.11), channel_id=2, replica_groups=mesh['zone'=32,'sub'=4] {'sub'}, dimensions={0}, use_global_device_ids=true | all-gather | bytes 163840 | tf_op jit(solution)/shard_map/all_gather | solution.py:21
  228.4 12.3 %all-to-all-start.4 = ((f32[32,2,512]{2,1,0:T(2,128)}), f32[32,2,512]{2,1,0:T(2,128)S(1)}, u32[]{:S(2)}, u32[]{:S(2)}) async-start(f32[32,2,512]{2,1,0:T(2,128)} %reshape.244), calls=%async_computation.4 | async-start | bytes 262144 | tf_op jit(solution)/shard_map/all_to_all | solution.py:202
  240.9 7.5 %all-to-all-done.4 = f32[32,2,512]{2,1,0:T(2,128)S(1)} async-done(((f32[32,2,512]{2,1,0:T(2,128)}), f32[32,2,512]{2,1,0:T(2,128)S(1)}, u32[]{:S(2)}, u32[]{:S(2)}) %all-to-all-start.4) | async-done | bytes 131104 | tf_op jit(solution)/shard_map/all_to_all | solution.py:202
  248.5 47.6 %while.74 = (s32[]{:T(128)}, f32[8,8,512]{2,1,0:T(8,128)S(1)}, f32[8,8,512]{2,1,0:T(8,128)S(1)}, pred[8,8,512]{2,1,0:T(8,128)(4,1)S(1)}, f32[8,8,512]{2,1,0:T(8,...) while((s32[]{:T(128)}, f32[8,8,512]{2,1,0:T(8,128)S(1)}, ...), condition=%wide.region_14.15_spmd, body=%wide.region_11.14_spmd.sunk | while | flops 559931392 | bytes 19072096 | solution.py:105
  296.3 47.2 %while.75 = (s32[]{:T(128)}, f32[8,8,512]{2,1,0:T(8,128)S(1)}, f32[8,8,512]{2,1,0:T(8,128)S(1)}, pred[8,8,512]{2,1,0:T(8,128)(4,1)S(1)}, f32[8,8,512]{2,1,0:T(8,...) while((s32[]{:T(128)}, f32[8,8,512]{2,1,0:T(8,128)S(1)}, ...), condition=%wide.region_20.21_spmd, body=%wide.region_17.20_spmd.sunk | while | flops 559931392 | bytes 19072096 | solution.py:105
  348.8 7.0 %all-to-all-done.5 = f32[32,2,512]{2,1,0:T(2,128)S(1)} async-done(((f32[32,2,512]{2,1,0:T(2,128)}), f32[32,2,512]{2,1,0:T(2,128)S(1)}, u32[]{:S(2)}, u32[]{:S(2)}) %all-to-all-start.5) | async-done | bytes 131104 | tf_op jit(solution)/shard_map/all_to_all | solution.py:180
  355.8 3.9 all-to-all-start.6
  360.2 7.2 %all-to-all-done.6 = f32[32,2,512]{2,1,0:T(2,128)S(1)} async-done(((f32[32,2,512]{2,1,0:T(2,128)}), f32[32,2,512]{2,1,0:T(2,128)S(1)}, u32[]{:S(2)}, u32[]{:S(2)}) %all-to-all-start.6) | async-done | bytes 131104 | tf_op jit(solution)/shard_map/all_to_all | solution.py:187
  368.1 9.3 %all-gather.3 = f32[64,512]{1,0:T(8,128)S(1)} all-gather(f32[16,512]{1,0:T(8,128)S(1)} %select_reduce_fusion.8), channel_id=5, replica_groups=mesh['zone'=32,'sub'=4] {'sub'}, dimensions={0}, use_global_device_ids=true | all-gather | bytes 163840 | tf_op jit(solution)/shard_map/all_gather | solution.py:21
  377.4 9.1 %all-gather.2 = f32[64,512]{1,0:T(8,128)S(1)} all-gather(f32[16,512]{1,0:T(8,128)S(1)} %select_reduce_fusion.9), channel_id=4, replica_groups=mesh['zone'=32,'sub'=4] {'sub'}, dimensions={0}, use_global_device_ids=true | all-gather | bytes 163840 | tf_op jit(solution)/shard_map/all_gather | solution.py:21
  388.2 9.5 %all-to-all-start.7 = ((f32[32,2,512]{2,1,0:T(2,128)}), f32[32,2,512]{2,1,0:T(2,128)S(1)}, u32[]{:S(2)}, u32[]{:S(2)}) async-start(f32[32,2,512]{2,1,0:T(2,128)} %reshape.247), calls=%async_computation.7 | async-start | bytes 262144 | tf_op jit(solution)/shard_map/all_to_all | solution.py:202
  398.3 7.1 %all-to-all-done.7 = f32[32,2,512]{2,1,0:T(2,128)S(1)} async-done(((f32[32,2,512]{2,1,0:T(2,128)}), f32[32,2,512]{2,1,0:T(2,128)S(1)}, u32[]{:S(2)}, u32[]{:S(2)}) %all-to-all-start.7) | async-done | bytes 131104 | tf_op jit(solution)/shard_map/all_to_all | solution.py:202
  405.6 47.6 %while.77 = (s32[]{:T(128)}, f32[8,8,512]{2,1,0:T(8,128)S(1)}, f32[8,8,512]{2,1,0:T(8,128)S(1)}, pred[8,8,512]{2,1,0:T(8,128)(4,1)S(1)}, f32[8,8,512]{2,1,0:T(8,...) while((s32[]{:T(128)}, f32[8,8,512]{2,1,0:T(8,128)S(1)}, ...), condition=%wide.region_28.29_spmd, body=%wide.region_25.28_spmd.sunk | while | flops 559931392 | bytes 19072096 | solution.py:105
  (236 shorter events, 203.1 us)
Async XLA Ops:
  0.6 1.6 copy-start
  18.2 9.4 %copy-start.3 = (s32[16]{0:T(128)S(1)}, s32[16]{0:T(128)}, u32[]{:S(2)}) copy-start(s32[16]{0:T(128)} %param.30) | copy-start | bytes 196
  18.2 108.5 %copy-start.2 = (bf16[512,128]{1,0:T(8,128)(2,1)S(1)}, bf16[512,128]{1,0:T(8,128)(2,1)}, u32[]{:S(2)}) copy-start(bf16[512,128]{1,0:T(8,128)(2,1)} %param.27) | copy-start | bytes 393220
  18.2 108.5 %all-to-all-start.1 = ((bf16[32,2,512,128]{3,2,1,0:T(8,128)(2,1)}), bf16[32,2,512,128]{3,2,1,0:T(8,128)(2,1)}, u32[]{:S(2)}, u32[]{:S(2)}) async-start(bf16[32,2,512,128]{3,2,1,0:T(8,128)(2,1)} %bitcast.158), calls=%async_computation.1 | async-start | bytes 16777216 | tf_op jit(solution)/shard_map/all_to_all | solution.py:158
  172.4 17.7 %all-to-all-start.2 = ((f32[32,2,512]{2,1,0:T(2,128)}), f32[32,2,512]{2,1,0:T(2,128)S(1)}, u32[]{:S(2)}, u32[]{:S(2)}) async-start(f32[32,2,512]{2,1,0:T(2,128)} %reshape_reshape.29), calls=%async_computation.2 | async-start | bytes 262144 | tf_op jit(solution)/shard_map/all_to_all | solution.py:180
  190.1 11.7 %all-to-all-start.3 = ((f32[32,2,512]{2,1,0:T(2,128)}), f32[32,2,512]{2,1,0:T(2,128)S(1)}, u32[]{:S(2)}, u32[]{:S(2)}) async-start(f32[32,2,512]{2,1,0:T(2,128)} %reshape_reshape.30), calls=%async_computation.3 | async-start | bytes 262144 | tf_op jit(solution)/shard_map/all_to_all | solution.py:187
  201.8 26.7 %all-to-all-start = ((bf16[32,2,512]{2,1,0:T(2,128)(2,1)}), bf16[32,2,512]{2,1,0:T(2,128)(2,1)S(1)}, u32[]{:S(2)}, u32[]{:S(2)}) async-start(bf16[32,2,512]{2,1,0:T(2,128)(2,1)} %and_convert_fusion), calls=%async_computation | async-start | bytes 131072 | tf_op jit(solution)/shard_map/all_to_all | solution.py:159
  228.4 19.9 %all-to-all-start.4 = ((f32[32,2,512]{2,1,0:T(2,128)}), f32[32,2,512]{2,1,0:T(2,128)S(1)}, u32[]{:S(2)}, u32[]{:S(2)}) async-start(f32[32,2,512]{2,1,0:T(2,128)} %reshape.244), calls=%async_computation.4 | async-start | bytes 262144 | tf_op jit(solution)/shard_map/all_to_all | solution.py:202
  248.5 47.7 %copy-start.4 = (bf16[512]{0:T(512)(128)(2,1)S(1)}, bf16[512]{0:T(512)(128)(2,1)}, u32[]{:S(2)}) copy-start(bf16[512]{0:T(512)(128)(2,1)} %param.28) | copy-start | bytes 3076
  344.2 11.6 %all-to-all-start.5 = ((f32[32,2,512]{2,1,0:T(2,128)}), f32[32,2,512]{2,1,0:T(2,128)S(1)}, u32[]{:S(2)}, u32[]{:S(2)}) async-start(f32[32,2,512]{2,1,0:T(2,128)} %reshape_reshape.32), calls=%async_computation.5 | async-start | bytes 262144 | tf_op jit(solution)/shard_map/all_to_all | solution.py:180
  355.8 11.7 %all-to-all-start.6 = ((f32[32,2,512]{2,1,0:T(2,128)}), f32[32,2,512]{2,1,0:T(2,128)S(1)}, u32[]{:S(2)}, u32[]{:S(2)}) async-start(f32[32,2,512]{2,1,0:T(2,128)} %reshape_reshape.33), calls=%async_computation.6 | async-start | bytes 262144 | tf_op jit(solution)/shard_map/all_to_all | solution.py:187
  388.2 17.3 %all-to-all-start.7 = ((f32[32,2,512]{2,1,0:T(2,128)}), f32[32,2,512]{2,1,0:T(2,128)S(1)}, u32[]{:S(2)}, u32[]{:S(2)}) async-start(f32[32,2,512]{2,1,0:T(2,128)} %reshape.247), calls=%async_computation.7 | async-start | bytes 262144 | tf_op jit(solution)/shard_map/all_to_all | solution.py:202
  453.2 1.6 copy-start.1
where the time goes:
time: 456 us; the launch traced here: 455 us
  waiting for transfers between devices  140 us (31%)
  matrix products  108 us (24%)
  other arithmetic  85.1 us (19%)
  starting transfers between devices  56.1 us (12%)
  blocking collectives  38.8 us (9%)
  local copies, waits for them, and re-layouts  23 us (5%)
    dot_general x32, matrix products, one_group(): jnp.einsum('tie,tje->tij', order_part, courier_part, preferred_element_ty...  99.1 us
    all_to_all x1, waiting for transfers between devices, shards(): lax.all_to_all(sent[0], 'zone', split_axis=0, concat_axis=0, tiled=True)  97.2 us
    reduce_sum x32, other arithmetic, one_group(): jnp.sum(jnp.where(usable, jnp.exp(pair_scores - running_highest), 0.0), a...  80.5 us
    all_gather x4, blocking collectives, combined_all(): pieces = jax.tree.map(lambda part: lax.all_gather(part, axis), value)  38.8 us
    all_to_all x2, starting transfers between devices, shards(): lax.all_to_all(order_potentials[source].reshape(zone_count, CB_DEV * per_...  21.8 us
    all_to_all x2, waiting for transfers between devices, shards(): lax.all_to_all(order_potentials[source].reshape(zone_count, CB_DEV * per_...  14.6 us
    all_to_all x2, waiting for transfers between devices, shards(): lax.all_to_all(summed_terms.reshape(zone_count, CB_DEV * per_source, BLOC...  14.5 us
    all_to_all x2, waiting for transfers between devices, shards(): lax.all_to_all(running_highest.reshape(zone_count, CB_DEV * per_source, B...  14 us
  transfers between devices with their start and end apart: 8, of which 7 were waited for; matrix products, arithmetic and copies ran while one was open for 2% of the time, Pallas kernels for 0%

commit v1 on v0

v1 whole, which is shorter than its diff:
```python
import math

import jax
import jax.numpy as jnp
from jax import lax
from jax.experimental import pallas as pl
from jax.experimental.pallas import tpu as pltpu
from jax.sharding import PartitionSpec as P

BLOCK = 512
EMB = 128
HID = 512
ADJ = 8
OB_DEV = 16
ZONES = 32
SUBS = 4
HALF = 256
UNROLL = 4
MOST_ENTRIES = 256
LIST_SIZE = MOST_ENTRIES + 2 * UNROLL
NO_ORDER = 2 * OB_DEV
NO_COURIER = 2 * ZONES

TEMPER = 0.2
LOWEST = -1e30
SCORE_SCALE = math.log2(math.e) / (TEMPER * math.sqrt(EMB))
DUAL_SCALE = TEMPER * math.log(2.0)

VMEM_LIMIT = 40 * 1024 * 1024


def zone_of(y, x, core):
    return ((y % 4) * 4 + (x % 4)) * 2 + core


PLACES = [(y, x, core) for y in range(4) for x in range(4) for core in range(2)]


def along_x(value, step):
    return lax.ppermute(value, "zone", [(zone_of(y, x, c), zone_of(y, x + step, c)) for y, x, c in PLACES])


def along_y(value, step):
    return lax.ppermute(value, "zone", [(zone_of(y, x, c), zone_of(y + step, x, c)) for y, x, c in PLACES])


def other_core(value):
    return lax.ppermute(value, "zone", [(zone_of(y, x, c), zone_of(y, x, 1 - c)) for y, x, c in PLACES])


def along_z(value, step):
    return lax.ppermute(value, "sub", [(i, (i + step) % SUBS) for i in range(SUBS)])


def join(*parts):
    highest = parts[0]
    for part in parts[1:]:
        highest = jnp.maximum(highest, part)
    total = jnp.exp2(parts[0] - highest)
    for part in parts[1:]:
        total = total + jnp.exp2(part - highest)
    return highest + jnp.log2(total)


def join_subs(value):
    return join(value, along_z(value, 1), along_z(value, 2), along_z(value, 3))


def join_zones(value):
    value = join(value, other_core(value))
    value = join(value, along_x(value, 1), along_x(value, 2), along_x(value, 3))
    return join(value, along_y(value, 1), along_y(value, 2), along_y(value, 3))


def embed_kernel(count_ref, x_ref, w_in_ref, b_in_ref, w_out_ref, b_out_ref, o_ref):
    block = pl.program_id(0)
    count = count_ref[block]
    for half in range(2):

        @pl.when(count > half * HALF)
        def _():
            rows = pl.ds(half * HALF, HALF)
            v = jnp.dot(x_ref[rows, :], w_in_ref[...], preferred_element_type=jnp.float32)
            v = 0.5 * (v + b_in_ref[...])
            hidden = (v + v * jnp.tanh(v)).astype(jnp.bfloat16)
            out = jnp.dot(hidden, w_out_ref[...], preferred_element_type=jnp.float32)
            o_ref[rows, :] = ((out + b_out_ref[...]) * SCORE_SCALE).astype(jnp.bfloat16)


def embed_orders(count, features, w_in, bias_in, w_out, bias_out):
    whole = lambda i, c: (0, 0)
    return pl.pallas_call(
        embed_kernel,
        out_shape=jax.ShapeDtypeStruct((OB_DEV * BLOCK, EMB), jnp.bfloat16),
        grid_spec=pltpu.PrefetchScalarGridSpec(
            num_scalar_prefetch=1,
            grid=(OB_DEV,),
            in_specs=[
                pl.BlockSpec((BLOCK, EMB), lambda i, c: (i, 0)),
                pl.BlockSpec((EMB, HID), whole),
                pl.BlockSpec((1, HID), whole),
                pl.BlockSpec((HID, EMB), whole),
                pl.BlockSpec((1, EMB), whole),
            ],
            out_specs=pl.BlockSpec((BLOCK, EMB), lambda i, c: (i, 0)),
        ),
        cost_estimate=pl.CostEstimate(flops=2 * 2 * 8192 * 128 * 512, bytes_accessed=5 << 20, transcendentals=8192 * 512),
        name="embed_orders",
    )(count, features, w_in, bias_in.reshape(1, HID), w_out, bias_out.reshape(1, EMB))


def list_kernel(adj_ref, order_count_ref, courier_count_ref, sub_ref, list_ref, rounds_ref):
    sub = sub_ref[0]

    def put(n, order, courier, keep):
        list_ref[n] = order * 256 + courier
        return n + keep

    def one_pair(p, n):
        b = p // ADJ
        c = adj_ref[p]
        z = c // SUBS
        mine = jnp.where(c % SUBS == sub, 1, 0)
        order_two = mine * jnp.where(order_count_ref[b] > HALF, 1, 0)
        courier_two = mine * jnp.where(courier_count_ref[z] > HALF, 1, 0)
        n = put(n, 2 * b, 2 * z, mine)
        n = put(n, 2 * b, 2 * z + 1, courier_two)
        n = put(n, 2 * b + 1, 2 * z, order_two)
        return put(n, 2 * b + 1, 2 * z + 1, order_two * courier_two)

    n = lax.fori_loop(0, OB_DEV * ADJ, one_pair, jnp.int32(0))
    for i in range(UNROLL):
        list_ref[n + i] = jnp.int32(NO_ORDER * 256 + NO_COURIER)
    rounds_ref[0] = (n + UNROLL - 1) // UNROLL


def work_list(adjacency, order_count, courier_count, sub):
    smem = pl.BlockSpec(memory_space=pltpu.SMEM)
    return pl.pallas_call(
        list_kernel,
        out_shape=(
            jax.ShapeDtypeStruct((LIST_SIZE,), jnp.int32),
            jax.ShapeDtypeStruct((1,), jnp.int32),
        ),
        in_specs=[smem] * 4,
        out_specs=(smem, smem),
        name="work_list",
    )(adjacency.reshape(-1), order_count, courier_count, sub.reshape(1))


def pass_kernel(sum_couriers, list_ref, rounds_ref, summed_ref, kept_ref, weight_ref, live_ref, out_ref, w_ref, r_ref, m_ref):
    summed_blocks, kept_blocks = weight_ref.shape[0], live_ref.shape[0]
    rounds = rounds_ref[0]

    def piece(e):
        order, courier = e // 256, e % 256
        return (courier, order) if sum_couriers else (order, courier)

    def scores(s, k):
        s = jnp.minimum(s, 2 * summed_blocks - 1)
        k = jnp.minimum(k, 2 * kept_blocks - 1)
        left = summed_ref[pl.ds(pl.multiple_of(s * HALF, HALF), HALF), :]
        right = kept_ref[pl.ds(pl.multiple_of(k * HALF, HALF), HALF), :]
        return lax.dot_general(left, right, (((1,), (1,)), ((), ())), preferred_element_type=jnp.float32)

    weight = weight_ref[...]
    linear = jnp.exp2(weight)
    high = linear.astype(jnp.bfloat16).astype(jnp.float32)
    low = linear - high
    row = lax.broadcasted_iota(jnp.int32, (summed_blocks, 16, HALF), 1)
    for half in range(2):
        cut = slice(half * HALF, (half + 1) * HALF)
        rows = jnp.where(row == 0, high[:, None, cut], jnp.where(row == 1, low[:, None, cut], 0.0))
        w_ref[0:summed_blocks, half] = rows.astype(jnp.bfloat16)
    w_ref[summed_blocks] = jnp.zeros((2, 16, HALF), jnp.bfloat16)
    r_ref[...] = jnp.zeros(r_ref.shape, jnp.float32)

    def one_round(i, carry):
        todo = [piece(list_ref[i * UNROLL + t]) for t in range(UNROLL)]
        sums = []
        for s, k in todo:
            terms = jnp.exp2(scores(s, k)).astype(jnp.bfloat16)
            sums.append(jnp.dot(w_ref[s // 2, s % 2], terms, preferred_element_type=jnp.float32)[0:8])
        for (s, k), part in zip(todo, sums):
            r_ref[k // 2, k % 2] += part
        return carry

    lax.fori_loop(0, rounds, one_round, 0)

    is_live_weight = weight > 0.5 * LOWEST
    highest = jnp.max(weight)
    lowest = jnp.min(jnp.where(is_live_weight, weight, 0.0))
    least = jnp.exp2(jnp.full((1, 1), jnp.clip(highest, 0.0, 100.0) - 86.0, jnp.float32))
    bad = jnp.where((highest <= 100.0) & (lowest >= -100.0), 0.0, 1.0)
    for half in range(2):
        cut = slice(half * HALF, (half + 1) * HALF)
        total = r_ref[0:kept_blocks, half, 0, :] + r_ref[0:kept_blocks, half, 1, :]
        live = live_ref[:, cut] > 0.5 * LOWEST
        fine = (total >= least) & (total <= 2.0**126)
        bad = bad + jnp.max(jnp.where(live, jnp.where(fine, 0.0, 1.0), 0.0))
        out_ref[:, cut] = jnp.where(live, jnp.log2(jnp.where(live, total, 1.0)), LOWEST)

    @pl.when(bad > 0.0)
    def _():
        m_ref[...] = jnp.full(m_ref.shape, LOWEST, jnp.float32)
        r_ref[...] = jnp.zeros(r_ref.shape, jnp.float32)

        def one_piece(i, carry):
            s, k = piece(list_ref[i])
            block = jnp.minimum(s // 2, summed_blocks - 1)
            w = weight_ref[pl.ds(block, 1), pl.ds(pl.multiple_of((s % 2) * HALF, HALF), HALF)]
            column = jnp.transpose(jnp.broadcast_to(w, (128, HALF)))
            x = scores(s, k) + jnp.concatenate([column, column], axis=1)
            before = m_ref[k // 2, k % 2, 0:1]
            after = jnp.maximum(before, jnp.max(x, axis=0, keepdims=True))
            scaled = r_ref[k // 2, k % 2, 0:1] * jnp.exp2(before - after)
            m_ref[k // 2, k % 2, 0:1] = after
            r_ref[k // 2, k % 2, 0:1] = scaled + jnp.sum(jnp.exp2(x - after), axis=0, keepdims=True)
            return carry

        lax.fori_loop(0, rounds * UNROLL, one_piece, 0)
        for half in range(2):
            cut = slice(half * HALF, (half + 1) * HALF)
            live = live_ref[:, cut] > 0.5 * LOWEST
            total = jnp.where(live, r_ref[0:kept_blocks, half, 0, :], 1.0)
            out_ref[:, cut] = jnp.where(live, m_ref[0:kept_blocks, half, 0, :] + jnp.log2(total), LOWEST)


def half_sweep(sum_couriers, work, rounds, summed, kept, weight, live, name):
    smem = pl.BlockSpec(memory_space=pltpu.SMEM)
    vmem = pl.BlockSpec(memory_space=pltpu.VMEM)
    summed_blocks, kept_blocks = weight.shape[0], live.shape[0]

    def kernel(*refs):
        pass_kernel(sum_couriers, *refs)

    return pl.pallas_call(
        kernel,
        out_shape=jax.ShapeDtypeStruct((kept_blocks, BLOCK), jnp.float32),
        in_specs=[smem, smem, vmem, vmem, vmem, vmem],
        out_specs=vmem,
        scratch_shapes=[
            pltpu.VMEM((summed_blocks + 1, 2, 16, HALF), jnp.bfloat16),
            pltpu.VMEM((kept_blocks + 1, 2, 8, HALF), jnp.float32),
            pltpu.VMEM((kept_blocks + 1, 2, 8, HALF), jnp.float32),
        ],
        compiler_params=pltpu.CompilerParams(vmem_limit_bytes=VMEM_LIMIT),
        cost_estimate=pl.CostEstimate(flops=28 * 2 * 512 * 512 * 128, bytes_accessed=6 << 20, transcendentals=28 * 512 * 512),
        name=name,
    )(work, rounds, summed, kept, weight, live)


def shards(
    order_features,
    w_in,
    bias_in,
    w_out,
    bias_out,
    courier_embed,
    courier_cap,
    adjacency,
    order_count,
    courier_count,
):
    sub = lax.axis_index("sub")
    positions = jnp.arange(BLOCK, dtype=jnp.int32)

    couriers = lax.all_gather(courier_embed, "zone", tiled=True)
    own_log_cap = jnp.where(
        positions < courier_count[0], jnp.log2(courier_cap.astype(jnp.float32)), LOWEST
    )
    log_cap = lax.all_to_all(
        jnp.broadcast_to(own_log_cap[None], (ZONES, BLOCK)), "zone", 0, 0, tiled=True
    )
    courier_live = log_cap > 0.5 * LOWEST
    counts = jnp.sum(courier_live.astype(jnp.int32), axis=1)

    orders = embed_orders(order_count, order_features, w_in, bias_in, w_out, bias_out)
    work, rounds = work_list(adjacency, order_count, counts, sub)

    mine = adjacency % SUBS == sub
    order_live = positions[None, :] < order_count[:, None]
    order_here = jnp.where(order_live & jnp.any(mine, axis=1, keepdims=True), 0.0, LOWEST)
    named = jnp.any(
        (adjacency.reshape(-1)[None, :] == jnp.arange(ZONES)[:, None] * SUBS + sub), axis=1, keepdims=True
    )
    courier_here = jnp.where(courier_live & named, 0.0, LOWEST)

    def order_pass(courier_dual, name):
        partial = half_sweep(True, work, rounds, couriers, orders, courier_dual, order_here, name)
        return jnp.where(order_live, -join_subs(partial), LOWEST)

    def courier_pass(order_dual, name):
        return half_sweep(False, work, rounds, orders, couriers, order_dual, courier_here, name)

    courier_dual = jnp.where(courier_live, 0.0, LOWEST)
    order_dual = order_pass(courier_dual, "orders_1")
    sums = join_zones(courier_pass(order_dual, "couriers_1"))
    courier_dual = jnp.where(courier_live, log_cap - sums, LOWEST)
    order_dual = order_pass(courier_dual, "orders_2")
    partial = courier_pass(order_dual, "couriers_2")
    parts = lax.all_to_all(partial, "zone", 0, 0, tiled=True)
    highest = jnp.max(parts, axis=0)
    total = highest + jnp.log2(jnp.sum(jnp.exp2(parts - highest[None]), axis=0))
    courier_out = jnp.where(positions < courier_count[0], DUAL_SCALE * (own_log_cap - total), 0.0)
    order_out = jnp.where(order_live, DUAL_SCALE * order_dual, 0.0)
    return order_out.reshape(-1), courier_out


def solution(mesh):
    return jax.shard_map(
        shards,
        mesh=mesh,
        in_specs=(
            P("zone", None),
            P(),
            P(),
            P(),
            P(),
            P(("zone", "sub"), None),
            P(("zone", "sub")),
            P("zone", None),
            P("zone"),
            P(("zone", "sub")),
        ),
        out_specs=(P("zone"), P(("zone", "sub"))),
        check_vma=False,
    )
```

time: 456 us -> 340 us (0.75)
  the two profiles are of different devices: /device:TPU:1 before, /device:TPU:33 now
where the time goes in v1:
time: 340 us; the launch traced here: 335 us
  Pallas kernels  218 us (64%)
  starting transfers between devices  47 us (14%)
  waiting for transfers between devices  44.2 us (13%)
  between operations  14.9 us (4%)
  local copies, waits for them, and re-layouts  7.29 us (2%)
  other arithmetic  3.49 us (1%)
    pallas_call x4, Pallas kernels, half_sweep(): pl.pallas_call(kernel, out_shape=jax.ShapeDtypeStruct((kept_blocks, BLOCK...  198 us
    all_to_all x1, starting transfers between devices, shards(): parts = lax.all_to_all(partial, 'zone', 0, 0, tiled=True)  18.9 us
    all_gather x1, waiting for transfers between devices, shards(): couriers = lax.all_gather(courier_embed, 'zone', tiled=True)  18.8 us
    pallas_call x1, Pallas kernels, embed_orders(): pl.pallas_call(embed_kernel, out_shape=jax.ShapeDtypeStruct((OB_DEV * BLO...  15.5 us
    ppermute x1, starting transfers between devices, other_core(): lax.ppermute(value, 'zone', [(zone_of(y, x, c), zone_of(y, x, 1 - c)) for...  14.2 us
    all_to_all x1, starting transfers between devices, shards(): lax.all_to_all(jnp.broadcast_to(own_log_cap[None], (ZONES, BLOCK)), 'zone...  7.76 us
    ppermute x6, waiting for transfers between devices, along_z(): lax.ppermute(value, 'sub', [(i, (i + step) % SUBS) for i in range(SUBS)])  6.87 us
    all_to_all x1, waiting for transfers between devices, shards(): parts = lax.all_to_all(partial, 'zone', 0, 0, tiled=True)  6.81 us
  transfers between devices with their start and end apart: 16, of which 15 were waited for; matrix products, arithmetic and copies ran while one was open for 1% of the time, Pallas kernels for 6%

profile of v1, /device:TPU:33, one launch (start us, length us, event | category | flops | bytes accessed | tf_op | source)
XLA Modules:
  0.0 334.8 jit_solution(7371492212234642143)
XLA Ops:
  9.9 7.8 %all-to-all-start = ((f32[32,1,512]{2,1,0:T(1,128)}), f32[32,1,512]{2,1,0:T(1,128)S(1)}, u32[]{:S(2)}, u32[]{:S(2)}) async-start(f32[32,1,512]{2,1,0:T(1,128)} %broadcast_in_dim.44), calls=%async_computation | async-start | bytes 131072 | tf_op jit(solution)/shard_map/all_to_all | solution.py:272
  19.2 15.5 %embed_orders.1.refs_3_.refs_2_ = bf16[8192,128]{1,0:T(8,128)(2,1)} custom-call(s32[16]{0:T(128)} %count_ref.1, bf16[8192,128]{1,0:T(8,128)(2,1)} %x_ref.1, bf16[128,512]{1,0:T(8,128)(2,1)} %w_in_ref.1, f32[1,512]{1,0:T(1,128)} %bitcast.26, bf16[512,128]{1,0:T(8,128)(2,1)} %w_out_ref.1, f32[1,128]{1,0:T(1,128)} %bitcast.27), custom_call_target="tpu_custom_call" | custom-call | flops 2147483648 | bytes 5242880 | tf_op jit(solution)/shard_map/embed_orders/pallas_call | solution.py:92
  35.8 4.1 %work_list.1 = (s32[264]{0:T(512)}, s32[1]{0:T(128)}) custom-call(s32[128]{0:T(128)} %copy-done.6, s32[16]{0:T(128)} %count_ref.1, s32[32]{0:T(128)} %convert_reduce_fusion.courier_count_ref, s32[1]{0:T(128)} %bitcast.1.sub_ref), custom_call_target="tpu_custom_call" | custom-call | tf_op jit(solution)/shard_map/work_list/pallas_call | solution.py:139
  39.9 18.8 %all-gather.2.cloned.1.call-done.refs_2_.refs_3_ = bf16[16384,128]{1,0:T(8,128)(2,1)} async-done(((bf16[512,128]{1,0:T(8,128)(2,1)}), bf16[16384,128]{1,0:T(8,128)(2,1)}) %all-gather.2.cloned.1.call-update) | async-done | bytes 4194320 | tf_op jit(solution)/shard_map/all_gather | solution.py:268
  58.7 2.2 copy-done
  61.6 1.6 copy-done.2
  63.2 49.6 %orders_1.1 = f32[16,512]{1,0:T(8,128)S(1)} custom-call(s32[264]{0:T(512)S(1)} %copy-done.1, s32[1]{0:T(128)} %get-tuple-element.5.refs_1_, bf16[16384,128]{1,0:T(8,128)(2,1)S(1)} %copy-done, bf16[8192,128]{1,0:T(8,128)(2,1)S(1)} %copy-done.2, f32[32,512]{1,0:T(8,128)S(1)} %broadcast_select_fusion.refs_4_, f32[16,512]{1,0:T(8,128)S(1)} %fusion.7.refs_5_), custom_call_target="tpu_custom_call" | custom-call | flops 1879048192 | bytes 6291456 | tf_op jit(solution)/shard_map/orders_1/pallas_call | solution.py:237
  112.9 1.4 collective-permute-start
  115.6 1.6 collective-permute-done.1
  117.8 49.6 %couriers_1.1 = f32[32,512]{1,0:T(8,128)S(1)} custom-call(s32[264]{0:T(512)S(1)} %copy-done.1, s32[1]{0:T(128)} %get-tuple-element.5.refs_1_, bf16[8192,128]{1,0:T(8,128)(2,1)S(1)} %copy-done.2, bf16[16384,128]{1,0:T(8,128)(2,1)S(1)} %copy-done, f32[16,512]{1,0:T(8,128)S(1)} %negate_select_fusion.1.refs_4_, f32[32,512]{1,0:T(8,128)S(1)} %get-tuple-element.8.refs_5_), custom_call_target="tpu_custom_call" | custom-call | flops 1879048192 | bytes 6291456 | tf_op jit(solution)/shard_map/couriers_1/pallas_call | solution.py:237
  167.4 14.2 %collective-permute-start.3 = (f32[32,512]{1,0:T(8,128)S(1)}, f32[32,512]{1,0:T(8,128)S(1)}, u32[]{:S(2)}, u32[]{:S(2)}) collective-permute-start(f32[32,512]{1,0:T(8,128)S(1)} %couriers_1.1), channel_id=1, source_target_pairs={{0,4},{4,0},{8,12},{12,8},{16,20},{20,16},{24,28},{28,24},{32,36},... | collective-permute-start | bytes 196616 | tf_op jit(solution)/shard_map/ppermute | solution.py:48
  182.8 1.4 collective-permute-start.4
  184.2 1.6 collective-permute-done.6
  185.8 1.6 collective-permute-done.5
  187.4 2.1 collective-permute-done.4
  189.7 1.4 collective-permute-start.7
  191.1 1.6 collective-permute-done.9
  192.8 1.6 collective-permute-done.8
  194.4 1.6 collective-permute-done.7
  196.0 49.6 %orders_2.1 = f32[16,512]{1,0:T(8,128)S(1)} custom-call(s32[264]{0:T(512)S(1)} %copy-done.1, s32[1]{0:T(128)} %get-tuple-element.5.refs_1_, bf16[16384,128]{1,0:T(8,128)(2,1)S(1)} %copy-done, bf16[8192,128]{1,0:T(8,128)(2,1)S(1)} %copy-done.2, f32[32,512]{1,0:T(8,128)S(1)} %fusion.3.refs_4_, f32[16,512]{1,0:T(8,128)S(1)} %fusion.7.refs_5_), custom_call_target="tpu_custom_call" | custom-call | flops 1879048192 | bytes 6291456 | tf_op jit(solution)/shard_map/orders_2/pallas_call | solution.py:237
  248.4 1.6 collective-permute-done.11
  250.6 49.6 %couriers_2.1 = f32[32,512]{1,0:T(8,128)S(1)} custom-call(s32[264]{0:T(512)S(1)} %copy-done.1, s32[1]{0:T(128)} %get-tuple-element.5.refs_1_, bf16[8192,128]{1,0:T(8,128)(2,1)S(1)} %copy-done.2, bf16[16384,128]{1,0:T(8,128)(2,1)S(1)} %copy-done, f32[16,512]{1,0:T(8,128)S(1)} %get-tuple-element.7.refs_4_, f32[32,512]{1,0:T(8,128)S(1)} %get-tuple-element.8.refs_5_), custom_call_target="tpu_custom_call" | custom-call | flops 1879048192 | bytes 6291456 | tf_op jit(solution)/shard_map/couriers_2/pallas_call | solution.py:237
  301.0 18.9 %all-to-all-start.1 = ((f32[32,1,512]{2,1,0:T(1,128)}), f32[32,1,512]{2,1,0:T(1,128)S(1)}, u32[]{:S(2)}, u32[]{:S(2)}) async-start(f32[32,1,512]{2,1,0:T(1,128)} %copy.17), calls=%async_computation.1 | async-start | bytes 131072 | tf_op jit(solution)/shard_map/all_to_all | solution.py:302
  320.4 6.8 %all-to-all-done.1 = f32[32,1,512]{2,1,0:T(1,128)S(1)} async-done(((f32[32,1,512]{2,1,0:T(1,128)}), f32[32,1,512]{2,1,0:T(1,128)S(1)}, u32[]{:S(2)}, u32[]{:S(2)}) %all-to-all-start.1) | async-done | bytes 65568 | tf_op jit(solution)/shard_map/all_to_all | solution.py:302
  (50 shorter events, 14.3 us)
Async XLA Ops:
  7.2 51.5 %all-gather.2.cloned.1.call-start = ((), (), s32[]{:S(2)}) async-start(), calls=%async_computation.2 | async-start | bytes 4325376 | tf_op jit(solution)/shard_map/all_gather | solution.py:268
  9.9 25.2 %all-to-all-start = ((f32[32,1,512]{2,1,0:T(1,128)}), f32[32,1,512]{2,1,0:T(1,128)S(1)}, u32[]{:S(2)}, u32[]{:S(2)}) async-start(f32[32,1,512]{2,1,0:T(1,128)} %broadcast_in_dim.44), calls=%async_computation | async-start | bytes 131072 | tf_op jit(solution)/shard_map/all_to_all | solution.py:272
  18.5 16.3 %copy-start.6 = (s32[128]{0:T(128)}, s32[128]{0:T(128)S(1)}, u32[]{:S(2)}) copy-start(s32[128]{0:T(128)S(1)} %reshape.39.adj_ref) | copy-start | bytes 1540
  19.2 15.5 %copy-start.3 = (s32[16]{0:T(128)S(1)}, s32[16]{0:T(128)}, u32[]{:S(2)}) copy-start(s32[16]{0:T(128)} %count_ref.1) | copy-start | bytes 196
  58.7 2.2 copy-start
  60.9 0.7 copy-start.1
  61.6 1.6 copy-start.2
  63.2 54.6 %copy-start.4 = (s32[16]{0:T(128)S(1)}, s32[16]{0:T(128)}, u32[]{:S(2)}) copy-start(s32[16]{0:T(128)} %count_ref.1) | copy-start | bytes 196
  112.7 2.8 collective-permute-start.2
  112.8 4.3 %collective-permute-start.1 = (f32[16,512]{1,0:T(8,128)S(1)}, f32[16,512]{1,0:T(8,128)S(1)}, u32[]{:S(2)}, u32[]{:S(2)}) collective-permute-start(f32[16,512]{1,0:T(8,128)S(1)} %orders_1.1), channel_id=1, source_target_pairs={{0,2},{1,3},{2,0},{3,1},{4,6},{5,7},{6,4},{7,5},{8,10},{9,11},{10,... | collective-permute-start | bytes 98312 | tf_op jit(solution)/shard_map/ppermute | solution.py:52
  112.9 4.8 %collective-permute-start = (f32[16,512]{1,0:T(8,128)S(1)}, f32[16,512]{1,0:T(8,128)S(1)}, u32[]{:S(2)}, u32[]{:S(2)}) collective-permute-start(f32[16,512]{1,0:T(8,128)S(1)} %orders_1.1), channel_id=1, source_target_pairs={{0,1},{1,2},{2,3},{3,0},{4,5},{5,6},{6,7},{7,4},{8,9},{9,10},{10,1... | collective-permute-start | bytes 98312 | tf_op jit(solution)/shard_map/ppermute | solution.py:52
  167.4 15.1 %collective-permute-start.3 = (f32[32,512]{1,0:T(8,128)S(1)}, f32[32,512]{1,0:T(8,128)S(1)}, u32[]{:S(2)}, u32[]{:S(2)}) collective-permute-start(f32[32,512]{1,0:T(8,128)S(1)} %couriers_1.1), channel_id=1, source_target_pairs={{0,4},{4,0},{8,12},{12,8},{16,20},{20,16},{24,28},{28,24},{32,36},... | collective-permute-start | bytes 196616 | tf_op jit(solution)/shard_map/ppermute | solution.py:48
  182.6 3.2 collective-permute-start.6
  182.7 4.7 %collective-permute-start.5 = (f32[32,512]{1,0:T(8,128)S(1)}, f32[32,512]{1,0:T(8,128)S(1)}, u32[]{:S(2)}, u32[]{:S(2)}) collective-permute-start(f32[32,512]{1,0:T(8,128)S(1)} %multiply_add_fusion.1), channel_id=1, source_target_pairs={{0,16},{4,20},{8,24},{12,28},{16,0},{20,4},{24,8},{28,12},{32,48},... | collective-permute-start | bytes 196616 | tf_op jit(solution)/shard_map/ppermute | solution.py:40
  182.8 6.7 %collective-permute-start.4 = (f32[32,512]{1,0:T(8,128)S(1)}, f32[32,512]{1,0:T(8,128)S(1)}, u32[]{:S(2)}, u32[]{:S(2)}) collective-permute-start(f32[32,512]{1,0:T(8,128)S(1)} %multiply_add_fusion.1), channel_id=1, source_target_pairs={{0,8},{4,12},{8,16},{12,20},{16,24},{20,28},{24,0},{28,4},{32,40},... | collective-permute-start | bytes 196616 | tf_op jit(solution)/shard_map/ppermute | solution.py:40
  189.6 3.2 collective-permute-start.9
  189.7 4.7 %collective-permute-start.8 = (f32[32,512]{1,0:T(8,128)S(1)}, f32[32,512]{1,0:T(8,128)S(1)}, u32[]{:S(2)}, u32[]{:S(2)}) collective-permute-start(f32[32,512]{1,0:T(8,128)S(1)} %multiply_add_fusion), channel_id=1, source_target_pairs={{0,64},{4,68},{8,72},{12,76},{16,80},{20,84},{24,88},{28,92},{32,9... | collective-permute-start | bytes 196616 | tf_op jit(solution)/shard_map/ppermute | solution.py:44
  189.7 6.2 %collective-permute-start.7 = (f32[32,512]{1,0:T(8,128)S(1)}, f32[32,512]{1,0:T(8,128)S(1)}, u32[]{:S(2)}, u32[]{:S(2)}) collective-permute-start(f32[32,512]{1,0:T(8,128)S(1)} %multiply_add_fusion), channel_id=1, source_target_pairs={{0,32},{4,36},{8,40},{12,44},{16,48},{20,52},{24,56},{28,60},{32,6... | collective-permute-start | bytes 196616 | tf_op jit(solution)/shard_map/ppermute | solution.py:44
  245.6 2.8 collective-permute-start.12
  245.7 4.3 %collective-permute-start.11 = (f32[16,512]{1,0:T(8,128)S(1)}, f32[16,512]{1,0:T(8,128)S(1)}, u32[]{:S(2)}, u32[]{:S(2)}) collective-permute-start(f32[16,512]{1,0:T(8,128)S(1)} %orders_2.1), channel_id=1, source_target_pairs={{0,2},{1,3},{2,0},{3,1},{4,6},{5,7},{6,4},{7,5},{8,10},{9,11},{10,... | collective-permute-start | bytes 98312 | tf_op jit(solution)/shard_map/ppermute | solution.py:52
  245.7 4.8 %collective-permute-start.10 = (f32[16,512]{1,0:T(8,128)S(1)}, f32[16,512]{1,0:T(8,128)S(1)}, u32[]{:S(2)}, u32[]{:S(2)}) collective-permute-start(f32[16,512]{1,0:T(8,128)S(1)} %orders_2.1), channel_id=1, source_target_pairs={{0,1},{1,2},{2,3},{3,0},{4,5},{5,6},{6,7},{7,4},{8,9},{9,10},{10,1... | collective-permute-start | bytes 98312 | tf_op jit(solution)/shard_map/ppermute | solution.py:52
  250.6 76.7 %copy-start.5 = (bf16[512]{0:T(512)(128)(2,1)S(1)}, bf16[512]{0:T(512)(128)(2,1)}, u32[]{:S(2)}) copy-start(bf16[512]{0:T(512)(128)(2,1)} %param.16) | copy-start | bytes 3076
  301.0 26.3 %all-to-all-start.1 = ((f32[32,1,512]{2,1,0:T(1,128)}), f32[32,1,512]{2,1,0:T(1,128)S(1)}, u32[]{:S(2)}, u32[]{:S(2)}) async-start(f32[32,1,512]{2,1,0:T(1,128)} %copy.17), calls=%async_computation.1 | async-start | bytes 131072 | tf_op jit(solution)/shard_map/all_to_all | solution.py:302
Sparse Core Ops, SparseCore 0:
  10.3 48.3 all-gather.1

commit v2 on v1

--- a/solution.py
+++ b/solution.py
@@ -15,9 +15,10 @@
 ZONES = 32
 SUBS = 4
 HALF = 256
-UNROLL = 4
+UNROLL = 16
+REST = 4
 MOST_ENTRIES = 256
-LIST_SIZE = MOST_ENTRIES + 2 * UNROLL
+LIST_SIZE = MOST_ENTRIES + 2 * REST
 NO_ORDER = 2 * OB_DEV
 NO_COURIER = 2 * ZONES
 
@@ -72,41 +73,40 @@
     return join(value, along_y(value, 1), along_y(value, 2), along_y(value, 3))
 
 
-def embed_kernel(count_ref, x_ref, w_in_ref, b_in_ref, w_out_ref, b_out_ref, o_ref):
-    block = pl.program_id(0)
-    count = count_ref[block]
-    for half in range(2):
-
-        @pl.when(count > half * HALF)
-        def _():
-            rows = pl.ds(half * HALF, HALF)
-            v = jnp.dot(x_ref[rows, :], w_in_ref[...], preferred_element_type=jnp.float32)
-            v = 0.5 * (v + b_in_ref[...])
-            hidden = (v + v * jnp.tanh(v)).astype(jnp.bfloat16)
-            out = jnp.dot(hidden, w_out_ref[...], preferred_element_type=jnp.float32)
-            o_ref[rows, :] = ((out + b_out_ref[...]) * SCORE_SCALE).astype(jnp.bfloat16)
-
-
-def embed_orders(count, features, w_in, bias_in, w_out, bias_out):
-    whole = lambda i, c: (0, 0)
+EMBED_ROWS = 2048
+
+
+def embed_kernel(x_ref, w_in_ref, b_in_ref, w_out_ref, b_out_ref, o_ref):
+    for start in range(0, EMBED_ROWS, BLOCK):
+        rows = pl.ds(start, BLOCK)
+        v = jnp.dot(x_ref[rows, :], w_in_ref[...], preferred_element_type=jnp.float32)
+        v = 0.5 * (v + b_in_ref[...])
+        hidden = (v + v * jnp.tanh(v)).astype(jnp.bfloat16)
+        out = jnp.dot(hidden, w_out_ref[...], preferred_element_type=jnp.float32)
+        o_ref[rows, :] = ((out + b_out_ref[...]) * SCORE_SCALE).astype(jnp.bfloat16)
+
+
+def embed_orders(features, w_in, bias_in, w_out, bias_out):
+    rows = features.shape[0]
+    whole = lambda i: (0, 0)
     return pl.pallas_call(
         embed_kernel,
-        out_shape=jax.ShapeDtypeStruct((OB_DEV * BLOCK, EMB), jnp.bfloat16),
-        grid_spec=pltpu.PrefetchScalarGridSpec(
-            num_scalar_prefetch=1,
-            grid=(OB_DEV,),
-            in_specs=[
-                pl.BlockSpec((BLOCK, EMB), lambda i, c: (i, 0)),
-                pl.BlockSpec((EMB, HID), whole),
-                pl.BlockSpec((1, HID), whole),
-                pl.BlockSpec((HID, EMB), whole),
-                pl.BlockSpec((1, EMB), whole),
-            ],
-            out_specs=pl.BlockSpec((BLOCK, EMB), lambda i, c: (i, 0)),
+        out_shape=jax.ShapeDtypeStruct((rows, EMB), jnp.bfloat16),
+        grid=(rows // EMBED_ROWS,),
+        in_specs=[
+            pl.BlockSpec((EMBED_ROWS, EMB), lambda i: (i, 0)),
+            pl.BlockSpec((EMB, HID), whole),
+            pl.BlockSpec((1, HID), whole),
+            pl.BlockSpec((HID, EMB), whole),
+            pl.BlockSpec((1, EMB), whole),
+        ],
+        out_specs=pl.BlockSpec((EMBED_ROWS, EMB), lambda i: (i, 0)),
+        compiler_params=pltpu.CompilerParams(vmem_limit_bytes=VMEM_LIMIT),
+        cost_estimate=pl.CostEstimate(
+            flops=4 * rows * EMB * HID, bytes_accessed=4 * rows * EMB, transcendentals=rows * HID
         ),
-        cost_estimate=pl.CostEstimate(flops=2 * 2 * 8192 * 128 * 512, bytes_accessed=5 << 20, transcendentals=8192 * 512),
         name="embed_orders",
-    )(count, features, w_in, bias_in.reshape(1, HID), w_out, bias_out.reshape(1, EMB))
+    )(features, w_in, bias_in.reshape(1, HID), w_out, bias_out.reshape(1, EMB))
 
 
 def list_kernel(adj_ref, order_count_ref, courier_count_ref, sub_ref, list_ref, rounds_ref):
@@ -129,9 +129,9 @@
         return put(n, 2 * b + 1, 2 * z + 1, order_two * courier_two)
 
     n = lax.fori_loop(0, OB_DEV * ADJ, one_pair, jnp.int32(0))
-    for i in range(UNROLL):
+    for i in range(REST):
         list_ref[n + i] = jnp.int32(NO_ORDER * 256 + NO_COURIER)
-    rounds_ref[0] = (n + UNROLL - 1) // UNROLL
+    rounds_ref[0] = (n + REST - 1) // REST
 
 
 def work_list(adjacency, order_count, courier_count, sub):
@@ -151,52 +151,69 @@
 def pass_kernel(sum_couriers, list_ref, rounds_ref, summed_ref, kept_ref, weight_ref, live_ref, out_ref, w_ref, r_ref, m_ref):
     summed_blocks, kept_blocks = weight_ref.shape[0], live_ref.shape[0]
     rounds = rounds_ref[0]
+    weight = weight_ref[...]
+
+    high = weight.astype(jnp.bfloat16).astype(jnp.float32)
+    low = weight - high
+    blank = jnp.zeros((64 - 2 * summed_blocks, 128), jnp.float32)
+    for part in range(2):
+        rows = []
+        for value in (high, low):
+            rows += [value[:, part * 128 : part * 128 + 128], value[:, HALF + part * 128 : HALF + part * 128 + 128]]
+            if summed_blocks < 32:
+                rows.append(blank)
+        w_ref[part * 128 : part * 128 + 128, :] = jnp.transpose(jnp.concatenate(rows, axis=0)).astype(jnp.bfloat16)
+    r_ref[...] = jnp.zeros(r_ref.shape, jnp.float32)
+    lanes = lax.broadcasted_iota(jnp.int32, (1, 128), 1) % 64
 
     def piece(e):
         order, courier = e // 256, e % 256
         return (courier, order) if sum_couriers else (order, courier)
 
-    def scores(s, k):
+    def sides(s, k):
         s = jnp.minimum(s, 2 * summed_blocks - 1)
         k = jnp.minimum(k, 2 * kept_blocks - 1)
         left = summed_ref[pl.ds(pl.multiple_of(s * HALF, HALF), HALF), :]
         right = kept_ref[pl.ds(pl.multiple_of(k * HALF, HALF), HALF), :]
+        return left, right
+
+    def scores(left, right):
         return lax.dot_general(left, right, (((1,), (1,)), ((), ())), preferred_element_type=jnp.float32)
 
-    weight = weight_ref[...]
-    linear = jnp.exp2(weight)
-    high = linear.astype(jnp.bfloat16).astype(jnp.float32)
-    low = linear - high
-    row = lax.broadcasted_iota(jnp.int32, (summed_blocks, 16, HALF), 1)
+    def weighted(s, k):
+        left, right = sides(s, k)
+        lane = (s % 2) * summed_blocks + s // 2
+        ones = jnp.where(lanes == lane, 1.0, 0.0).astype(jnp.bfloat16)
+        left = jnp.concatenate([left, w_ref[...]], axis=1)
+        right = jnp.concatenate([right, jnp.broadcast_to(ones, (HALF, 128))], axis=1)
+        return scores(left, right)
+
+    def steps(first, count):
+        todo = [piece(list_ref[first + t]) for t in range(count)]
+        sums = [jnp.sum(jnp.exp2(weighted(s, k)).reshape(HALF // 8, 8, HALF), axis=0) for s, k in todo]
+        for (s, k), part in zip(todo, sums):
+            r_ref[k // 2, k % 2] += part
+
+    large = rounds // (UNROLL // REST)
+
+    def large_step(i, carry):
+        steps(i * UNROLL, UNROLL)
+        return carry
+
+    def small_step(i, carry):
+        steps(i * REST, REST)
+        return carry
+
+    lax.fori_loop(0, large, large_step, 0)
+    lax.fori_loop(large * (UNROLL // REST), rounds, small_step, 0)
+
+    live_weight = jnp.where(weight > 0.5 * LOWEST, jnp.abs(weight), 0.0)
+    bad = jnp.where(jnp.max(live_weight) <= 128.0, 0.0, 1.0)
     for half in range(2):
         cut = slice(half * HALF, (half + 1) * HALF)
-        rows = jnp.where(row == 0, high[:, None, cut], jnp.where(row == 1, low[:, None, cut], 0.0))
-        w_ref[0:summed_blocks, half] = rows.astype(jnp.bfloat16)
-    w_ref[summed_blocks] = jnp.zeros((2, 16, HALF), jnp.bfloat16)
-    r_ref[...] = jnp.zeros(r_ref.shape, jnp.float32)
-
-    def one_round(i, carry):
-        todo = [piece(list_ref[i * UNROLL + t]) for t in range(UNROLL)]
-        sums = []
-        for s, k in todo:
-            terms = jnp.exp2(scores(s, k)).astype(jnp.bfloat16)
-            sums.append(jnp.dot(w_ref[s // 2, s % 2], terms, preferred_element_type=jnp.float32)[0:8])
-        for (s, k), part in zip(todo, sums):
-            r_ref[k // 2, k % 2] += part
-        return carry
-
-    lax.fori_loop(0, rounds, one_round, 0)
-
-    is_live_weight = weight > 0.5 * LOWEST
-    highest = jnp.max(weight)
-    lowest = jnp.min(jnp.where(is_live_weight, weight, 0.0))
-    least = jnp.exp2(jnp.full((1, 1), jnp.clip(highest, 0.0, 100.0) - 86.0, jnp.float32))
-    bad = jnp.where((highest <= 100.0) & (lowest >= -100.0), 0.0, 1.0)
-    for half in range(2):
-        cut = slice(half * HALF, (half + 1) * HALF)
-        total = r_ref[0:kept_blocks, half, 0, :] + r_ref[0:kept_blocks, half, 1, :]
+        total = jnp.sum(r_ref[0:kept_blocks, half], axis=1)
         live = live_ref[:, cut] > 0.5 * LOWEST
-        fine = (total >= least) & (total <= 2.0**126)
+        fine = (total >= 2.0**-86) & (total <= 2.0**126)
         bad = bad + jnp.max(jnp.where(live, jnp.where(fine, 0.0, 1.0), 0.0))
         out_ref[:, cut] = jnp.where(live, jnp.log2(jnp.where(live, total, 1.0)), LOWEST)
 
@@ -210,7 +227,7 @@
             block = jnp.minimum(s // 2, summed_blocks - 1)
             w = weight_ref[pl.ds(block, 1), pl.ds(pl.multiple_of((s % 2) * HALF, HALF), HALF)]
             column = jnp.transpose(jnp.broadcast_to(w, (128, HALF)))
-            x = scores(s, k) + jnp.concatenate([column, column], axis=1)
+            x = scores(*sides(s, k)) + jnp.concatenate([column, column], axis=1)
             before = m_ref[k // 2, k % 2, 0:1]
             after = jnp.maximum(before, jnp.max(x, axis=0, keepdims=True))
             scaled = r_ref[k // 2, k % 2, 0:1] * jnp.exp2(before - after)
@@ -218,7 +235,7 @@
             r_ref[k // 2, k % 2, 0:1] = scaled + jnp.sum(jnp.exp2(x - after), axis=0, keepdims=True)
             return carry
 
-        lax.fori_loop(0, rounds * UNROLL, one_piece, 0)
+        lax.fori_loop(0, rounds * REST, one_piece, 0)
         for half in range(2):
             cut = slice(half * HALF, (half + 1) * HALF)
             live = live_ref[:, cut] > 0.5 * LOWEST
@@ -240,7 +257,7 @@
         in_specs=[smem, smem, vmem, vmem, vmem, vmem],
         out_specs=vmem,
         scratch_shapes=[
-            pltpu.VMEM((summed_blocks + 1, 2, 16, HALF), jnp.bfloat16),
+            pltpu.VMEM((HALF, 128), jnp.bfloat16),
             pltpu.VMEM((kept_blocks + 1, 2, 8, HALF), jnp.float32),
             pltpu.VMEM((kept_blocks + 1, 2, 8, HALF), jnp.float32),
         ],
@@ -275,7 +292,7 @@
     courier_live = log_cap > 0.5 * LOWEST
     counts = jnp.sum(courier_live.astype(jnp.int32), axis=1)
 
-    orders = embed_orders(order_count, order_features, w_in, bias_in, w_out, bias_out)
+    orders = embed_orders(order_features, w_in, bias_in, w_out, bias_out)
     work, rounds = work_list(adjacency, order_count, counts, sub)
 
     mine = adjacency % SUBS == sub

time: 340 us -> 263 us (0.77)
  the two profiles are of different devices: /device:TPU:33 before, /device:TPU:1 now
where the time goes in v2:
time: 263 us; the launch traced here: 266 us
  Pallas kernels  118 us (45%)
  starting transfers between devices  72.9 us (28%)
  waiting for transfers between devices  46.3 us (18%)
  between operations  14.9 us (6%)
  local copies, waits for them, and re-layouts  10.4 us (4%)
  other arithmetic  3.5 us (1%)
    pallas_call x4, Pallas kernels, half_sweep(): pl.pallas_call(kernel, out_shape=jax.ShapeDtypeStruct((kept_blocks, BLOCK...  108 us
    all_to_all x1, starting transfers between devices, shards(): parts = lax.all_to_all(partial, 'zone', 0, 0, tiled=True)  30.5 us
    all_gather x1, waiting for transfers between devices, shards(): couriers = lax.all_gather(courier_embed, 'zone', tiled=True)  23.9 us
    ppermute x1, starting transfers between devices, other_core(): lax.ppermute(value, 'zone', [(zone_of(y, x, c), zone_of(y, x, 1 - c)) for...  11.5 us
    unnamed x24, local copies, waits for them, and re-layouts  9.01 us
    all_to_all x1, starting transfers between devices, shards(): lax.all_to_all(jnp.broadcast_to(own_log_cap[None], (ZONES, BLOCK)), 'zone...  8.59 us
    ppermute x3, starting transfers between devices, along_x(): lax.ppermute(value, 'zone', [(zone_of(y, x, c), zone_of(y, x + step, c))...  8.54 us
    ppermute x3, starting transfers between devices, along_y(): lax.ppermute(value, 'zone', [(zone_of(y, x, c), zone_of(y + step, x, c))...  6.97 us
  transfers between devices with their start and end apart: 16, of which 12 were waited for; matrix products, arithmetic and copies ran while one was open for 2% of the time, Pallas kernels for 4%

profile of v2, /device:TPU:1, one launch (start us, length us, event | category | flops | bytes accessed | tf_op | source)
XLA Modules:
  0.0 265.8 jit_solution(8702608494273830383)
XLA Ops:
  9.9 8.6 %all-to-all-start = ((f32[32,1,512]{2,1,0:T(1,128)}), f32[32,1,512]{2,1,0:T(1,128)S(1)}, u32[]{:S(2)}, u32[]{:S(2)}) async-start(f32[32,1,512]{2,1,0:T(1,128)} %broadcast_in_dim.44), calls=%async_computation | async-start | bytes 131072 | tf_op jit(solution)/shard_map/all_to_all | solution.py:289
  20.1 1.6 copy-done.1
  22.6 0.9 copy-done.3
  24.8 6.0 %embed_orders.1.refs_3_.refs_2_ = bf16[8192,128]{1,0:T(8,128)(2,1)S(1)} custom-call(bf16[8192,128]{1,0:T(8,128)(2,1)S(1)} %copy-done.1, bf16[128,512]{1,0:T(8,128)(2,1)S(1)} %copy-done.2, f32[1,512]{1,0:T(1,128)S(1)} %bitcast.25, bf16[512,128]{1,0:T(8,128)(2,1)S(1)} %copy-done.3, f32[1,128]{1,0:T(1,128)S(1)} %bitcast.26), custom_call_target="tpu_custom_call" | custom-call | flops 2147483648 | bytes 4194304 | tf_op jit(solution)/shard_map/embed_orders/pallas_call | solution.py:92
  31.9 4.1 %work_list.1 = (s32[264]{0:T(512)}, s32[1]{0:T(128)}) custom-call(s32[128]{0:T(128)} %copy-done.10, s32[16]{0:T(128)} %order_count_ref.1, s32[32]{0:T(128)} %convert_reduce_fusion.courier_count_ref, s32[1]{0:T(128)} %bitcast.1.sub_ref), custom_call_target="tpu_custom_call" | custom-call | tf_op jit(solution)/shard_map/work_list/pallas_call | solution.py:139
  36.0 23.9 %all-gather.2.cloned.1.call-done.refs_2_.refs_3_ = bf16[16384,128]{1,0:T(8,128)(2,1)} async-done(((bf16[512,128]{1,0:T(8,128)(2,1)}), bf16[16384,128]{1,0:T(8,128)(2,1)}) %all-gather.2.cloned.1.call-update) | async-done | bytes 4194320 | tf_op jit(solution)/shard_map/all_gather | solution.py:285
  59.9 2.2 copy-done
  62.7 26.9 %orders_1.1 = f32[16,512]{1,0:T(8,128)S(1)} custom-call(s32[264]{0:T(512)S(1)} %copy-done.5, s32[1]{0:T(128)} %get-tuple-element.5.refs_1_, bf16[16384,128]{1,0:T(8,128)(2,1)S(1)} %copy-done, bf16[8192,128]{1,0:T(8,128)(2,1)S(1)} %embed_orders.1.refs_3_.refs_2_, f32[32,512]{1,0:T(8,128)S(1)} %broadcast_select_fusion.refs_4_, f32[16,512]{1,0:T(8,128)S(1)} %fusion.7.refs_5_), custom_call_target="tpu_custom_call" | custom-call | flops 1879048192 | bytes 6291456 | tf_op jit(solution)/shard_map/orders_1/pallas_call | solution.py:254
  89.7 4.4 %collective-permute-start.1 = (f32[16,512]{1,0:T(8,128)S(1)}, f32[16,512]{1,0:T(8,128)S(1)}, u32[]{:S(2)}, u32[]{:S(2)}) collective-permute-start(f32[16,512]{1,0:T(8,128)S(1)} %orders_1.1), channel_id=1, source_target_pairs={{0,2},{1,3},{2,0},{3,1},{4,6},{5,7},{6,4},{7,5},{8,10},{9,11},{10,... | collective-permute-start | bytes 98312 | tf_op jit(solution)/shard_map/ppermute | solution.py:53
  95.4 2.7 %collective-permute-done = f32[16,512]{1,0:T(8,128)S(1)} collective-permute-done((f32[16,512]{1,0:T(8,128)S(1)}, f32[16,512]{1,0:T(8,128)S(1)}, u32[]{:S(2)}, u32[]{:S(2)}) %collective-permute-start) | collective-permute-done | bytes 32800 | tf_op jit(solution)/shard_map/ppermute | solution.py:53
  98.2 27.0 %couriers_1.1 = f32[32,512]{1,0:T(8,128)S(1)} custom-call(s32[264]{0:T(512)S(1)} %copy-done.5, s32[1]{0:T(128)} %get-tuple-element.5.refs_1_, bf16[8192,128]{1,0:T(8,128)(2,1)S(1)} %embed_orders.1.refs_3_.refs_2_, bf16[16384,128]{1,0:T(8,128)(2,1)S(1)} %copy-done, f32[16,512]{1,0:T(8,128)S(1)} %negate_select_fusion.1.refs_4_, ...), custom_call_target="tpu_custom_call" | custom-call | flops 1879048192 | bytes 6291456 | tf_op jit(solution)/shard_map/couriers_1/pallas_call | solution.py:254
  125.1 11.5 %collective-permute-start.3 = (f32[32,512]{1,0:T(8,128)S(1)}, f32[32,512]{1,0:T(8,128)S(1)}, u32[]{:S(2)}, u32[]{:S(2)}) collective-permute-start(f32[32,512]{1,0:T(8,128)S(1)} %couriers_1.1), channel_id=1, source_target_pairs={{0,4},{4,0},{8,12},{12,8},{16,20},{20,16},{24,28},{28,24},{32,36},... | collective-permute-start | bytes 196616 | tf_op jit(solution)/shard_map/ppermute | solution.py:49
  137.7 7.7 %collective-permute-start.5 = (f32[32,512]{1,0:T(8,128)S(1)}, f32[32,512]{1,0:T(8,128)S(1)}, u32[]{:S(2)}, u32[]{:S(2)}) collective-permute-start(f32[32,512]{1,0:T(8,128)S(1)} %multiply_add_fusion.1), channel_id=1, source_target_pairs={{0,16},{4,20},{8,24},{12,28},{16,0},{20,4},{24,8},{28,12},{32,48},... | collective-permute-start | bytes 196616 | tf_op jit(solution)/shard_map/ppermute | solution.py:41
  146.1 1.4 collective-permute-done.5
  147.6 2.1 collective-permute-done.4
  149.9 6.1 %collective-permute-start.8 = (f32[32,512]{1,0:T(8,128)S(1)}, f32[32,512]{1,0:T(8,128)S(1)}, u32[]{:S(2)}, u32[]{:S(2)}) collective-permute-start(f32[32,512]{1,0:T(8,128)S(1)} %multiply_add_fusion), channel_id=1, source_target_pairs={{0,64},{4,68},{8,72},{12,76},{16,80},{20,84},{24,88},{28,92},{32,9... | collective-permute-start | bytes 196616 | tf_op jit(solution)/shard_map/ppermute | solution.py:45
  157.6 2.8 %collective-permute-done.7 = f32[32,512]{1,0:T(8,128)S(1)} collective-permute-done((f32[32,512]{1,0:T(8,128)S(1)}, f32[32,512]{1,0:T(8,128)S(1)}, u32[]{:S(2)}, u32[]{:S(2)}) %collective-permute-start.7) | collective-permute-done | bytes 65568 | tf_op jit(solution)/shard_map/ppermute | solution.py:45
  160.5 26.9 %orders_2.1 = f32[16,512]{1,0:T(8,128)S(1)} custom-call(s32[264]{0:T(512)S(1)} %copy-done.5, s32[1]{0:T(128)} %get-tuple-element.5.refs_1_, bf16[16384,128]{1,0:T(8,128)(2,1)S(1)} %copy-done, bf16[8192,128]{1,0:T(8,128)(2,1)S(1)} %embed_orders.1.refs_3_.refs_2_, f32[32,512]{1,0:T(8,128)S(1)} %fusion.3.refs_4_, f32[16,512]{1,0:T(8,128)S(1)} %fusion.7.refs_5_), custom_call_target="tpu_custom_call" | custom-call | flops 1879048192 | bytes 6291456 | tf_op jit(solution)/shard_map/orders_2/pallas_call | solution.py:254
  187.6 1.4 collective-permute-start.10
  188.9 1.3 collective-permute-done.12
  190.2 1.6 collective-permute-done.11
  192.7 27.0 %couriers_2.1 = f32[32,512]{1,0:T(8,128)S(1)} custom-call(s32[264]{0:T(512)S(1)} %copy-done.5, s32[1]{0:T(128)} %get-tuple-element.5.refs_1_, bf16[8192,128]{1,0:T(8,128)(2,1)S(1)} %embed_orders.1.refs_3_.refs_2_, bf16[16384,128]{1,0:T(8,128)(2,1)S(1)} %copy-done, f32[16,512]{1,0:T(8,128)S(1)} %get-tuple-element.7.refs_4_, ...), custom_call_target="tpu_custom_call" | custom-call | flops 1879048192 | bytes 6291456 | tf_op jit(solution)/shard_map/couriers_2/pallas_call | solution.py:254
  220.4 30.5 %all-to-all-start.1 = ((f32[32,1,512]{2,1,0:T(1,128)}), f32[32,1,512]{2,1,0:T(1,128)S(1)}, u32[]{:S(2)}, u32[]{:S(2)}) async-start(f32[32,1,512]{2,1,0:T(1,128)} %copy.17), calls=%async_computation.1 | async-start | bytes 131072 | tf_op jit(solution)/shard_map/all_to_all | solution.py:319
  251.5 6.7 %all-to-all-done.1 = f32[32,1,512]{2,1,0:T(1,128)S(1)} async-done(((f32[32,1,512]{2,1,0:T(1,128)}), f32[32,1,512]{2,1,0:T(1,128)S(1)}, u32[]{:S(2)}, u32[]{:S(2)}) %all-to-all-start.1) | async-done | bytes 65568 | tf_op jit(solution)/shard_map/all_to_all | solution.py:319
  (58 shorter events, 15.8 us)
Async XLA Ops:
  7.2 52.7 %all-gather.2.cloned.1.call-start = ((), (), s32[]{:S(2)}) async-start(), calls=%async_computation.2 | async-start | bytes 4325376 | tf_op jit(solution)/shard_map/all_gather | solution.py:285
  9.9 21.2 %all-to-all-start = ((f32[32,1,512]{2,1,0:T(1,128)}), f32[32,1,512]{2,1,0:T(1,128)S(1)}, u32[]{:S(2)}, u32[]{:S(2)}) async-start(f32[32,1,512]{2,1,0:T(1,128)} %broadcast_in_dim.44), calls=%async_computation | async-start | bytes 131072 | tf_op jit(solution)/shard_map/all_to_all | solution.py:289
  19.3 11.6 %copy-start.10 = (s32[128]{0:T(128)}, s32[128]{0:T(128)S(1)}, u32[]{:S(2)}) copy-start(s32[128]{0:T(128)S(1)} %reshape.39.adj_ref) | copy-start | bytes 1540
  20.1 1.6 copy-start.1
  21.7 0.9 copy-start.2
  22.6 0.9 copy-start.3
  24.8 6.0 %copy-start.7 = (s32[16]{0:T(128)S(1)}, s32[16]{0:T(128)}, u32[]{:S(2)}) copy-start(s32[16]{0:T(128)} %order_count_ref.1) | copy-start | bytes 196
  59.9 2.2 copy-start
  62.7 35.3 %copy-start.8 = (s32[16]{0:T(128)S(1)}, s32[16]{0:T(128)}, u32[]{:S(2)}) copy-start(s32[16]{0:T(128)} %order_count_ref.1) | copy-start | bytes 196
  89.6 5.2 %collective-permute-start.2 = (f32[16,512]{1,0:T(8,128)S(1)}, f32[16,512]{1,0:T(8,128)S(1)}, u32[]{:S(2)}, u32[]{:S(2)}) collective-permute-start(f32[16,512]{1,0:T(8,128)S(1)} %orders_1.1), channel_id=1, source_target_pairs={{0,3},{1,0},{2,1},{3,2},{4,7},{5,4},{6,5},{7,6},{8,11},{9,8},{10,9... | collective-permute-start | bytes 98312 | tf_op jit(solution)/shard_map/ppermute | solution.py:53
  89.7 5.7 %collective-permute-start.1 = (f32[16,512]{1,0:T(8,128)S(1)}, f32[16,512]{1,0:T(8,128)S(1)}, u32[]{:S(2)}, u32[]{:S(2)}) collective-permute-start(f32[16,512]{1,0:T(8,128)S(1)} %orders_1.1), channel_id=1, source_target_pairs={{0,2},{1,3},{2,0},{3,1},{4,6},{5,7},{6,4},{7,5},{8,10},{9,11},{10,... | collective-permute-start | bytes 98312 | tf_op jit(solution)/shard_map/ppermute | solution.py:53
  94.1 4.0 %collective-permute-start = (f32[16,512]{1,0:T(8,128)S(1)}, f32[16,512]{1,0:T(8,128)S(1)}, u32[]{:S(2)}, u32[]{:S(2)}) collective-permute-start(f32[16,512]{1,0:T(8,128)S(1)} %orders_1.1), channel_id=1, source_target_pairs={{0,1},{1,2},{2,3},{3,0},{4,5},{5,6},{6,7},{7,4},{8,9},{9,10},{10,1... | collective-permute-start | bytes 98312 | tf_op jit(solution)/shard_map/ppermute | solution.py:53
  125.1 12.4 %collective-permute-start.3 = (f32[32,512]{1,0:T(8,128)S(1)}, f32[32,512]{1,0:T(8,128)S(1)}, u32[]{:S(2)}, u32[]{:S(2)}) collective-permute-start(f32[32,512]{1,0:T(8,128)S(1)} %couriers_1.1), channel_id=1, source_target_pairs={{0,4},{4,0},{8,12},{12,8},{16,20},{20,16},{24,28},{28,24},{32,36},... | collective-permute-start | bytes 196616 | tf_op jit(solution)/shard_map/ppermute | solution.py:49
  137.6 8.5 %collective-permute-start.6 = (f32[32,512]{1,0:T(8,128)S(1)}, f32[32,512]{1,0:T(8,128)S(1)}, u32[]{:S(2)}, u32[]{:S(2)}) collective-permute-start(f32[32,512]{1,0:T(8,128)S(1)} %multiply_add_fusion.1), channel_id=1, source_target_pairs={{0,24},{4,28},{8,0},{12,4},{16,8},{20,12},{24,16},{28,20},{32,56},... | collective-permute-start | bytes 196616 | tf_op jit(solution)/shard_map/ppermute | solution.py:41
  137.7 9.9 %collective-permute-start.5 = (f32[32,512]{1,0:T(8,128)S(1)}, f32[32,512]{1,0:T(8,128)S(1)}, u32[]{:S(2)}, u32[]{:S(2)}) collective-permute-start(f32[32,512]{1,0:T(8,128)S(1)} %multiply_add_fusion.1), channel_id=1, source_target_pairs={{0,16},{4,20},{8,24},{12,28},{16,0},{20,4},{24,8},{28,12},{32,48},... | collective-permute-start | bytes 196616 | tf_op jit(solution)/shard_map/ppermute | solution.py:41
  145.4 4.3 %collective-permute-start.4 = (f32[32,512]{1,0:T(8,128)S(1)}, f32[32,512]{1,0:T(8,128)S(1)}, u32[]{:S(2)}, u32[]{:S(2)}) collective-permute-start(f32[32,512]{1,0:T(8,128)S(1)} %multiply_add_fusion.1), channel_id=1, source_target_pairs={{0,8},{4,12},{8,16},{12,20},{16,24},{20,28},{24,0},{28,4},{32,40},... | collective-permute-start | bytes 196616 | tf_op jit(solution)/shard_map/ppermute | solution.py:41
  149.8 7.0 %collective-permute-start.9 = (f32[32,512]{1,0:T(8,128)S(1)}, f32[32,512]{1,0:T(8,128)S(1)}, u32[]{:S(2)}, u32[]{:S(2)}) collective-permute-start(f32[32,512]{1,0:T(8,128)S(1)} %multiply_add_fusion), channel_id=1, source_target_pairs={{0,96},{4,100},{8,104},{12,108},{16,112},{20,116},{24,120},{28,124... | collective-permute-start | bytes 196616 | tf_op jit(solution)/shard_map/ppermute | solution.py:45
  149.9 7.8 %collective-permute-start.8 = (f32[32,512]{1,0:T(8,128)S(1)}, f32[32,512]{1,0:T(8,128)S(1)}, u32[]{:S(2)}, u32[]{:S(2)}) collective-permute-start(f32[32,512]{1,0:T(8,128)S(1)} %multiply_add_fusion), channel_id=1, source_target_pairs={{0,64},{4,68},{8,72},{12,76},{16,80},{20,84},{24,88},{28,92},{32,9... | collective-permute-start | bytes 196616 | tf_op jit(solution)/shard_map/ppermute | solution.py:45
  156.0 4.4 %collective-permute-start.7 = (f32[32,512]{1,0:T(8,128)S(1)}, f32[32,512]{1,0:T(8,128)S(1)}, u32[]{:S(2)}, u32[]{:S(2)}) collective-permute-start(f32[32,512]{1,0:T(8,128)S(1)} %multiply_add_fusion), channel_id=1, source_target_pairs={{0,32},{4,36},{8,40},{12,44},{16,48},{20,52},{24,56},{28,60},{32,6... | collective-permute-start | bytes 196616 | tf_op jit(solution)/shard_map/ppermute | solution.py:45
  187.4 2.8 %collective-permute-start.12 = (f32[16,512]{1,0:T(8,128)S(1)}, f32[16,512]{1,0:T(8,128)S(1)}, u32[]{:S(2)}, u32[]{:S(2)}) collective-permute-start(f32[16,512]{1,0:T(8,128)S(1)} %orders_2.1), channel_id=1, source_target_pairs={{0,3},{1,0},{2,1},{3,2},{4,7},{5,4},{6,5},{7,6},{8,11},{9,8},{10,9... | collective-permute-start | bytes 98312 | tf_op jit(solution)/shard_map/ppermute | solution.py:53
  187.5 4.3 %collective-permute-start.11 = (f32[16,512]{1,0:T(8,128)S(1)}, f32[16,512]{1,0:T(8,128)S(1)}, u32[]{:S(2)}, u32[]{:S(2)}) collective-permute-start(f32[16,512]{1,0:T(8,128)S(1)} %orders_2.1), channel_id=1, source_target_pairs={{0,2},{1,3},{2,0},{3,1},{4,6},{5,7},{6,4},{7,5},{8,10},{9,11},{10,... | collective-permute-start | bytes 98312 | tf_op jit(solution)/shard_map/ppermute | solution.py:53
  187.6 5.1 %collective-permute-start.10 = (f32[16,512]{1,0:T(8,128)S(1)}, f32[16,512]{1,0:T(8,128)S(1)}, u32[]{:S(2)}, u32[]{:S(2)}) collective-permute-start(f32[16,512]{1,0:T(8,128)S(1)} %orders_2.1), channel_id=1, source_target_pairs={{0,1},{1,2},{2,3},{3,0},{4,5},{5,6},{6,7},{7,4},{8,9},{9,10},{10,1... | collective-permute-start | bytes 98312 | tf_op jit(solution)/shard_map/ppermute | solution.py:53
  192.7 65.6 %copy-start.9 = (bf16[512]{0:T(512)(128)(2,1)S(1)}, bf16[512]{0:T(512)(128)(2,1)}, u32[]{:S(2)}) copy-start(bf16[512]{0:T(512)(128)(2,1)} %param.16) | copy-start | bytes 3076
  220.4 37.8 %all-to-all-start.1 = ((f32[32,1,512]{2,1,0:T(1,128)}), f32[32,1,512]{2,1,0:T(1,128)S(1)}, u32[]{:S(2)}, u32[]{:S(2)}) async-start(f32[32,1,512]{2,1,0:T(1,128)} %copy.17), calls=%async_computation.1 | async-start | bytes 131072 | tf_op jit(solution)/shard_map/all_to_all | solution.py:319
  (3 other events, 2.0 us)
Sparse Core Ops, SparseCore 0:
  10.3 49.5 all-gather.1
